TPU v7x, 128 devices: a whole 4x4x4 slice. The times are simulated.
128 devices in a mesh: ctx: 16 (over y, x), exp: 8 (over z, core).
Axes of the slice: x: 4, y: 4, z: 4, core: 2. Of those that a mesh axis runs over, the one named last changes fastest.
Arguments:
- queries: bfloat16 [4, 1024, 8192], P(None, 'ctx', 'exp'), may hold values from -2 to 2
- keys: bfloat16 [4, 1024, 8192], P(None, 'ctx', 'exp'), may hold values from -2 to 2
- values: bfloat16 [4, 1024, 8192], P(None, 'ctx', 'exp'), may hold values from -6 to 6
- decay_log: float32 [1024, 64], P('ctx', 'exp'), may hold values from -0.9 to 0
- out_gate: bfloat16 [4, 1024, 8192], P(None, 'ctx', 'exp'), may hold values from -6 to 6
- head_gain: float32 [8192], P('exp'), may hold values from 0.1 to 1.9
- out_weight: bfloat16 [8192, 6144], P('exp', 'ctx'), may hold values from -0.0625 to 0.0625
- stream: bfloat16 [4, 1024, 6144], P(None, ('ctx', 'exp')), may hold values from -6 to 6
- norm_gain: float32 [6144], replicated, may hold values from 0.1 to 1.9
- expert_ids: int32 [128, 32, 2], P(('ctx', 'exp')), may hold values from 0 to 7, all different within a row; in each aligned block of 32 rows (0 to 31, 32 to 63, ..., all dimensions but the last counted through in order) at most 9 rows name the same one
- expert_share: float32 [128, 32, 2], P(('ctx', 'exp')), may hold values from 0.2 to 1
- w_gate: bfloat16 [8, 6144, 9216], P('exp', None, 'ctx'), may hold values from -0.078125 to 0.078125
- w_up: bfloat16 [8, 6144, 9216], P('exp', None, 'ctx'), may hold values from -0.078125 to 0.078125
- w_down: bfloat16 [8, 9216, 6144], P('exp', 'ctx'), may hold values from -0.0625 to 0.0625
Outputs:
- layer_out: bfloat16 [4, 1024, 6144], P(None, ('ctx', 'exp'))
Inputs may be any that keep to these rules, and one draw needn't show every extreme that they name: `expert_ids`: within a routing group no expert takes more than 9 copies, some group gives one expert exactly 9, and the two picks of a token differ.
All inputs are finite; a program needn't handle non-finite values.
Results may differ from a plain program's by a relative error of at most 0.02.
Values may be sent and summed in bfloat16 or wider, within the bound.
A program may use at most 192 MiB of HBM per device.

v0:
```python
import jax
import jax.numpy as jnp
from jax import lax
from jax.experimental import pallas as pl
from jax.experimental.pallas import tpu as pltpu
from jax.sharding import Mesh, PartitionSpec as P

CTX = ("y", "x")
EXP = ("z", "c")


MESH = pl.DeviceIdType.MESH
AXES = (("x", "y"), ("y", "x"))


def greet(others):
    barrier = pltpu.get_barrier_semaphore()
    for where in others:
        pl.semaphore_signal(barrier, inc=1, device_id=where, device_id_type=MESH)
    pl.semaphore_wait(barrier, len(others))


def signal_others(others):
    barrier = pltpu.get_barrier_semaphore()
    for where in others:
        pl.semaphore_signal(barrier, inc=1, device_id=where, device_id_type=MESH)
    return barrier


def expert_place(t):
    return {"z": t // 2, "c": lax.rem(t, 2)}


def gather_kernel(
    main_ref,
    last_ref,
    wg_hbm,
    wu_hbm,
    hid_ref,
    buf_a,
    buf_b,
    rows_ref,
    wg,
    wu,
    xin,
    acc_g,
    acc_u,
    last_in,
    last_out,
    ssem,
    rsem,
    lsem,
    esend,
    erecv,
):
    n = 4
    experts, main, _ = main_ref.shape
    mine_e = lax.axis_index("z") * 2 + lax.axis_index("c")
    count, width = rows_ref.shape
    half = width // 2
    quarter = half // 2
    hidden = wg.shape[0]
    buf = (buf_a, buf_b)
    place = {a: lax.axis_index(a) for a in ("x", "y")}

    def step(axis, by):
        return lax.rem(place[axis] + (by + n), n)

    load_g = pltpu.make_async_copy(wg_hbm, wg, lsem.at[0])
    load_u = pltpu.make_async_copy(wu_hbm, wu, lsem.at[1])
    load_g.start()
    load_u.start()
    greet(
        [{a: step(a, d)} for a in ("x", "y") for d in (1, -1)]
        + [expert_place(lax.rem(mine_e + d, experts)) for d in range(1, experts)]
    )

    def main_rows(e):
        return rows_ref.at[pl.ds(pl.multiple_of(e * main, 8), main)]

    def deal(d, to, frm):
        return [
            pltpu.make_async_remote_copy(
                src_ref=src,
                dst_ref=dst,
                send_sem=esend.at[k, d],
                recv_sem=erecv.at[k, d],
                device_id=expert_place(to),
                device_id_type=MESH,
            )
            for k, (src, dst) in enumerate(
                ((main_ref.at[to], main_rows(frm)), (last_ref.at[to], last_in.at[frm]))
            )
        ]

    @pl.loop(1, experts)
    def _(d):
        for c in deal(d, lax.rem(mine_e + d, experts), mine_e):
            c.start()

    own_main = pltpu.make_async_copy(main_ref.at[mine_e], main_rows(mine_e), lsem.at[6])
    own_last = pltpu.make_async_copy(last_ref.at[mine_e], last_in.at[mine_e], lsem.at[7])
    own_main.start()
    own_last.start()
    acc_g[...] = jnp.zeros_like(acc_g)
    acc_u[...] = jnp.zeros_like(acc_u)
    own_main.wait()
    own_last.wait()

    @pl.loop(1, experts)
    def _(d):
        for c in deal(d, lax.rem(mine_e + d, experts), lax.rem(mine_e - d + experts, experts)):
            c.wait()

    last_out[...] = last_in[...].reshape(last_out.shape).astype(jnp.bfloat16)
    put_last = pltpu.make_async_copy(
        last_out, rows_ref.at[pl.ds(experts * main, experts)], lsem.at[6]
    )
    put_last.start()
    put_last.wait()

    def row(h, fi, si):
        return buf[h].at[fi, pl.ds(pl.multiple_of(si * count, 8), count)]

    def cut(ref, k):
        return ref.at[:, pl.ds((k - 2) * quarter, quarter)] if k >= 2 else ref

    def send(h, stage, kind, axis, src, dst):
        to = step(axis, 1 if kind % 2 == 0 else -1)
        c = pltpu.make_async_remote_copy(
            src_ref=cut(src, kind),
            dst_ref=cut(dst, kind),
            send_sem=ssem.at[h, stage, kind],
            recv_sem=rsem.at[h, stage, kind],
            device_id={axis: to},
            device_id_type=MESH,
        )
        c.start()
        sent.append(c)

    def arrived(h, stage, kind, axis, dst):
        pltpu.make_async_remote_copy(
            src_ref=cut(dst, kind),
            dst_ref=cut(dst, kind),
            send_sem=ssem.at[h, stage, kind],
            recv_sem=rsem.at[h, stage, kind],
            device_id={axis: step(axis, 1)},
            device_id_type=MESH,
        ).wait_recv()

    sent = []
    shift = (0, -1, 1, 2)
    own = [rows_ref.at[:, pl.ds(h * half, half)] for h in range(2)]
    keep = []
    for h in range(2):
        first, second = AXES[h]
        mine = row(h, place[first], place[second])
        for kind in range(2):
            send(h, n, kind, first, own[h], mine)
    for h in range(2):
        first, second = AXES[h]
        mine = row(h, place[first], place[second])
        for kind in range(2):
            send(h, 0, kind, second, own[h], mine)
        keep.append(pltpu.make_async_copy(own[h], mine, lsem.at[2 + h]))
        keep[h].start()

    def spread(h, j):
        first, second = AXES[h]
        here = row(h, step(first, shift[j]), place[second])
        for kind in range(2):
            send(h, j, kind, second, here, here)

    def pass_on(h, stage, kind):
        first, second = AXES[h]
        by = -1 if kind == 0 else 1
        if stage == n:
            here = row(h, step(first, by), place[second])
            axis = first
        else:
            here = row(h, step(first, shift[stage]), step(second, by))
            axis = second
        arrived(h, stage, kind, axis, here)
        send(h, stage, kind + 2, axis, here, here)

    def far(h, stage):
        first, second = AXES[h]
        if stage == n:
            here, axis = row(h, step(first, 2), place[second]), first
        else:
            here, axis = row(h, step(first, shift[stage]), step(second, 2)), second
        for kind in (2, 3):
            arrived(h, stage, kind, axis, here)

    def load(h, j):
        return pltpu.make_async_copy(
            buf[h].at[step(AXES[h][0], shift[j])], xin.at[h], lsem.at[4 + h]
        )

    def multiply(h, j):
        load(h, j).wait()
        fi = step(AXES[h][0], shift[j])
        for w, acc in ((wg, acc_g), (wu, acc_u)):
            got = lax.dot_general(
                xin[h],
                w[:, pl.ds(h * half, half)],
                (((1,), (1,)), ((), ())),
                preferred_element_type=jnp.float32,
            ).reshape(n, count, hidden)
            if h == 0:
                acc[fi] += got
            else:
                acc[:, fi] += got

    def activate(p, q):
        g = acc_g[p, q]
        out = (g / (1.0 + jnp.exp(-g)) * acc_u[p, q]).astype(jnp.bfloat16)
        hid_ref[p, q] = out.astype(jnp.float32)

    for kind in range(2):
        for h in range(2):
            pass_on(h, n, kind)
            spread(h, 1 + kind)
    for kind in range(2):
        for h in range(2):
            pass_on(h, 0, kind)
    for h in range(2):
        far(h, n)
        spread(h, 3)
    load_g.wait()
    load_u.wait()
    for j in range(n):
        if j + 1 < n:
            for kind in range(2):
                for h in range(2):
                    pass_on(h, j + 1, kind)
        for h in range(2):
            if j == 0:
                keep[h].wait()
            far(h, j)
            load(h, j).start()
        for h in range(2):
            multiply(h, j)
        if j == 2:

            @pl.loop(0, 9)
            def _(k):
                a, b = k // 3, lax.rem(k, 3)
                activate(step("x", a + a // 2), step("y", b + b // 2))

    @pl.loop(0, n)
    def _(k):
        activate(step("x", 2), step("y", k))

    @pl.loop(0, n - 1)
    def _(k):
        activate(step("x", k + k // 2), step("y", 2))

    for c in sent:
        c.wait_send()


def reduce_kernel(
    hid_ref,
    wd_hbm,
    back_main,
    back_last,
    wd,
    rows,
    t_a,
    t_b,
    r_opp,
    r_full,
    part,
    r_opp2,
    r_full2,
    out_main,
    out_last,
    ssem,
    rsem,
    lsem,
    esend,
    erecv,
):
    n = 4
    experts, main, width = out_main.shape
    count = experts * (main + 1)
    mine_e = lax.axis_index("z") * 2 + lax.axis_index("c")
    half = width // 2
    quarter = half // 2
    block = min(512, quarter)
    t = (t_a, t_b)
    place = {a: lax.axis_index(a) for a in ("x", "y")}

    def step(axis, by):
        return lax.rem(place[axis] + (by + n), n)

    load = pltpu.make_async_copy(wd_hbm, wd, lsem.at[0])
    load.start()
    others = [{a: step(a, d)} for a in ("x", "y") for d in (1, -1)]
    others += [expert_place(lax.rem(mine_e + d, experts)) for d in range(1, experts)]
    barrier = signal_others(others)
    load.wait()
    shift = (2, 1, -1, 0)
    sent = []

    def copy(h, stage, kind, axis, src, dst):
        return pltpu.make_async_remote_copy(
            src_ref=src,
            dst_ref=dst,
            send_sem=ssem.at[h, stage, kind],
            recv_sem=rsem.at[h, stage, kind],
            device_id={axis: step(axis, 1 if kind % 2 == 0 else -1)},
            device_id_type=MESH,
        )

    def send(*a):
        c = copy(*a)
        c.start()
        sent.append(c)

    def arrived(h, stage, kind, axis, dst):
        copy(h, stage, kind, axis, dst, dst).wait_recv()

    def multiply(h, j):
        lead = step(AXES[h][0], shift[j])
        taken = hid_ref[lead] if h == 0 else hid_ref[:, pl.ds(lead, 1)]
        rows[...] = taken.reshape(rows.shape).astype(jnp.bfloat16)

        @pl.loop(0, half // block)
        def _(b):
            at = pl.multiple_of(b * block, 128)
            got = jnp.dot(
                rows[...],
                wd[:, pl.ds(pl.multiple_of(h * half + at, 128), block)],
                preferred_element_type=jnp.float32,
            )
            t[h][j, :, :, pl.ds(at, block)] = got.reshape(n, count, block).astype(jnp.bfloat16)

    def far_out(h, j):
        ring = AXES[h][1]
        for k in range(2):
            send(
                h,
                j,
                k,
                ring,
                t[h].at[j, step(ring, 2), :, pl.ds(k * quarter, quarter)],
                r_opp.at[h, j, k],
            )

    def add_to(ref, k, other):
        @pl.loop(0, quarter // block)
        def _(b):
            at = pl.multiple_of(b * block, 128)
            cols = pl.ds(pl.multiple_of(k * quarter + at, 128), block)
            ref[:, cols] = (
                ref[:, cols].astype(jnp.float32) + other[:, pl.ds(at, block)].astype(jnp.float32)
            ).astype(jnp.bfloat16)

    def add_up(refs, at):
        s = refs[0][:, pl.ds(at, block)].astype(jnp.float32)
        for r in refs[1:]:
            s = s + r[:, pl.ds(at, block)].astype(jnp.float32)
        return s

    def total(dst, refs):
        @pl.loop(0, half // block)
        def _(b):
            at = pl.multiple_of(b * block, 128)
            dst[:, pl.ds(at, block)] = add_up(refs, at).astype(jnp.bfloat16)

    def settle(h, refs):
        @pl.loop(0, half // block)
        def _(b):
            at = pl.multiple_of(b * block, 128)
            cols = pl.ds(pl.multiple_of(h * half + at, 128), block)
            s = add_up(refs, at)
            out_main[:, :, cols] = (
                s[: experts * main].reshape(experts, main, block).astype(jnp.bfloat16)
            )
            out_last[:, :, cols] = s[experts * main :].reshape(experts, 1, block)

    def give(k, d, to, frm):
        if k == 2:
            src, dst = out_last.at[to], back_last.at[frm]
        else:
            cols = pl.ds(k * half, half)
            src, dst = out_main.at[to, :, cols], back_main.at[frm, :, cols]
        return pltpu.make_async_remote_copy(
            src_ref=src,
            dst_ref=dst,
            send_sem=esend.at[k, d],
            recv_sem=erecv.at[k, d],
            device_id=expert_place(to),
            device_id_type=MESH,
        )

    def near(h, j):
        ring = AXES[h][1]
        for k in range(2):
            arrived(h, j, k, ring, r_opp.at[h, j, k])
            mine = t[h].at[j, step(ring, 1 if k == 0 else -1)]
            add_to(mine, k, r_opp.at[h, j, k])
            send(h, j, 2 + k, ring, mine, r_full.at[h, j, k])

    def both(h, j):
        for k in range(2):
            arrived(h, j, 2 + k, AXES[h][1], r_full.at[h, j, k])

    def finish(h, j):
        both(h, j)
        total(
            part.at[h, j],
            [t[h].at[j, place[AXES[h][1]]], r_full.at[h, j, 0], r_full.at[h, j, 1]],
        )

    for j in range(2):
        for h in range(2):
            multiply(h, j)
            if j == 0 and h == 0:
                pl.semaphore_wait(barrier, len(others))
            far_out(h, j)
    for j in range(n):
        for h in range(2):
            near(h, j)
        if j + 2 < n:
            for h in range(2):
                multiply(h, j + 2)
                far_out(h, j + 2)
        if j == 1:
            for h in range(2):
                finish(h, 0)
                for k in range(2):
                    send(
                        h,
                        n,
                        k,
                        AXES[h][0],
                        part.at[h, 0, :, pl.ds(k * quarter, quarter)],
                        r_opp2.at[h, k],
                    )
    for j in (1, 2):
        for h in range(2):
            finish(h, j)
            k = j - 1
            arrived(h, n, k, AXES[h][0], r_opp2.at[h, k])
            add_to(part.at[h, j], k, r_opp2.at[h, k])
            send(h, n, 2 + k, AXES[h][0], part.at[h, j], r_full2.at[h, k])
    for h in range(2):
        both(h, 3)
        for k in range(2):
            arrived(h, n, 2 + k, AXES[h][0], r_full2.at[h, k])
        settle(
            h,
            [
                t[h].at[3, place[AXES[h][1]]],
                r_full.at[h, 3, 0],
                r_full.at[h, 3, 1],
                r_full2.at[h, 0],
                r_full2.at[h, 1],
            ],
        )

        @pl.loop(1, experts)
        def _(d):
            for k in (h,) if h == 0 else (1, 2):
                give(k, d, lax.rem(mine_e + d, experts), mine_e).start()

    back_main[mine_e] = out_main[mine_e]
    back_last[mine_e] = out_last[mine_e]

    @pl.loop(1, experts)
    def _(d):
        for k in range(3):
            give(
                k, d, lax.rem(mine_e + d, experts), lax.rem(mine_e - d + experts, experts)
            ).wait()

    for c in sent:
        c.wait_send()


def expert_terms(main_rows, last_rows, w_gate, w_up):
    n = 4
    experts, main, width = main_rows.shape
    count = experts * (main + 1)
    hidden = w_gate.shape[0]
    half = width // 2
    any_spec = pl.BlockSpec(memory_space=pl.ANY)
    vmem = pl.BlockSpec(memory_space=pltpu.VMEM)
    bf16 = jnp.bfloat16
    return pl.pallas_call(
        gather_kernel,
        out_shape=[
            jax.ShapeDtypeStruct((n, n, count, hidden), jnp.float32),
            jax.ShapeDtypeStruct((n, n * count, half), bf16),
            jax.ShapeDtypeStruct((n, n * count, half), bf16),
            jax.ShapeDtypeStruct((count, width), bf16),
        ],
        in_specs=[any_spec] * 4,
        out_specs=[vmem, any_spec, any_spec, any_spec],
        scratch_shapes=[
            pltpu.VMEM((hidden, width), bf16),
            pltpu.VMEM((hidden, width), bf16),
            pltpu.VMEM((2, n * count, half), bf16),
            pltpu.VMEM((n, n, count, hidden), jnp.float32),
            pltpu.VMEM((n, n, count, hidden), jnp.float32),
            pltpu.VMEM((experts, 1, width), jnp.float32),
            pltpu.VMEM((experts, width), bf16),
            pltpu.SemaphoreType.DMA((2, n + 1, 4)),
            pltpu.SemaphoreType.DMA((2, n + 1, 4)),
            pltpu.SemaphoreType.DMA((8,)),
            pltpu.SemaphoreType.DMA((2, experts)),
            pltpu.SemaphoreType.DMA((2, experts)),
        ],
        compiler_params=pltpu.CompilerParams(
            collective_id=1, has_side_effects=True, vmem_limit_bytes=60 << 20
        ),
        name="gather_experts",
    )(main_rows, last_rows, w_gate, w_up)[0]


def expert_sum(hid, w_down, experts):
    n = 4
    hidden, width = w_down.shape
    count = hid.shape[2]
    main = count // experts - 1
    half = width // 2
    any_spec = pl.BlockSpec(memory_space=pl.ANY)
    vmem = pl.BlockSpec(memory_space=pltpu.VMEM)
    bf16 = jnp.bfloat16
    return pl.pallas_call(
        reduce_kernel,
        out_shape=[
            jax.ShapeDtypeStruct((experts, main, width), bf16),
            jax.ShapeDtypeStruct((experts, 1, width), jnp.float32),
        ],
        in_specs=[vmem, any_spec],
        out_specs=[vmem, vmem],
        scratch_shapes=[
            pltpu.VMEM((hidden, width), bf16),
            pltpu.VMEM((n * count, hidden), bf16),
            pltpu.VMEM((n, n, count, half), bf16),
            pltpu.VMEM((n, n, count, half), bf16),
            pltpu.VMEM((2, n, 2, count, half // 2), bf16),
            pltpu.VMEM((2, n, 2, count, half), bf16),
            pltpu.VMEM((2, 3, count, half), bf16),
            pltpu.VMEM((2, 2, count, half // 2), bf16),
            pltpu.VMEM((2, 2, count, half), bf16),
            pltpu.VMEM((experts, main, width), bf16),
            pltpu.VMEM((experts, 1, width), jnp.float32),
            pltpu.SemaphoreType.DMA((2, n + 1, 4)),
            pltpu.SemaphoreType.DMA((2, n + 1, 4)),
            pltpu.SemaphoreType.DMA((1,)),
            pltpu.SemaphoreType.DMA((3, experts)),
            pltpu.SemaphoreType.DMA((3, experts)),
        ],
        compiler_params=pltpu.CompilerParams(
            collective_id=2, has_side_effects=True, vmem_limit_bytes=60 << 20
        ),
        name="sum_experts",
    )(hid, w_down)


def front_kernel(
    chunks,
    fades,
    q_ref,
    k_ref,
    v_ref,
    gate_ref,
    gain_ref,
    cum_ref,
    cum_t_ref,
    stream_ref,
    norm_gain_ref,
    slots_ref,
    weight,
    residual_ref,
    main_ref,
    last_ref,
    out_ref,
    got,
    got_fade,
    held,
    incoming,
    decay,
    inner,
    scale,
    spread_tok,
    own_tok,
    tok,
    w,
    prod,
    other,
    ring_opp,
    ring_full,
    done,
    asend,
    arecv,
    wsend,
    wrecv,
    ssem,
    rsem,
    lsem,
):
    n = 4
    blocks, per, head_dim, _ = chunks.shape
    seqs, length, feats = q_ref.shape
    heads = fades.shape[0]
    cores, zs, count, width = prod.shape[1:]
    sub = length // (cores * zs)
    half_f = feats // 2
    half = width // 2
    block = width // n
    x = lax.axis_index("x")
    y = lax.axis_index("y")
    z = lax.axis_index("z")
    c = lax.axis_index("c")
    me = y * n + x

    def xs(by):
        return lax.rem(x + (by + n), n)

    def yy(by):
        return lax.rem(y + (by + n), n)

    def zz(by):
        return lax.rem(z + (by + n), n)

    def where(t):
        return {"y": t // n, "x": lax.rem(t, n)}

    load = pltpu.make_async_copy(weight, w.at[y], lsem.at[0])
    load.start()
    barrier = pltpu.get_barrier_semaphore()

    @pl.loop(1, blocks)
    def _(d):
        pl.semaphore_signal(
            barrier, inc=1, device_id=where(lax.rem(me + d, blocks)), device_id_type=MESH
        )

    for there in ({"z": zz(1)}, {"z": zz(-1)}, {"c": 1 - c}):
        pl.semaphore_signal(barrier, inc=1, device_id=there, device_id_type=MESH)
    pl.semaphore_wait(barrier, blocks + 2)

    def state_copy(kind, d, src, dst, t):
        return pltpu.make_async_remote_copy(
            src_ref=src,
            dst_ref=dst,
            send_sem=asend.at[kind, d],
            recv_sem=arecv.at[kind, d],
            device_id=where(t),
            device_id_type=MESH,
        )

    def fade_of(t):
        return fades.at[pl.ds(lax.rem(t * per, heads), per)]

    @pl.loop(1, blocks)
    def _(d):
        t = lax.rem(me + d, blocks)
        state_copy(0, d, chunks.at[t], got.at[me], t).start()
        state_copy(1, d, fade_of(t), got_fade.at[me], t).start()

    got[me] = chunks[me]
    got_fade[me] = fade_of(me)[...]

    row = lax.broadcasted_iota(jnp.int32, (length, length), 0)
    col = lax.broadcasted_iota(jnp.int32, (length, length), 1)
    for h in range(heads):
        gap = cum_ref[:, h : h + 1] - cum_t_ref[h : h + 1, :]
        decay[h] = jnp.exp(jnp.where(row >= col, gap, -1e30))

    @pl.loop(0, seqs)
    def _(s):
        g = gate_ref[s].astype(jnp.float32)
        scale[s] = gain_ref[...] / (1.0 + jnp.exp(-g))
        for h in range(heads):
            cols = pl.ds(h * head_dim, head_dim)
            scores = lax.dot_general(
                q_ref[s, :, cols],
                k_ref[s, :, cols],
                (((1,), (1,)), ((), ())),
                preferred_element_type=jnp.float32,
            )
            mix = (scores * decay[h]).astype(jnp.bfloat16)
            inner[s, :, cols] = jnp.dot(
                mix, v_ref[s, :, cols], preferred_element_type=jnp.float32
            )

    @pl.loop(1, blocks)
    def _(d):
        t = lax.rem(me + d, blocks)
        frm = lax.rem(me - d + blocks, blocks)
        state_copy(0, d, chunks.at[t], got.at[frm], t).wait()
        state_copy(1, d, fade_of(t), got_fade.at[frm], t).wait()

    def advance(b, state):
        held[b] = state.astype(jnp.bfloat16)
        d = lax.rem(b - me + blocks, blocks)

        @pl.when(d != 0)
        def _():
            state_copy(2, d, held.at[b], incoming.at[me], b).start()

        return got_fade[b][:, :1, :] * state + got[b].astype(jnp.float32)

    lax.fori_loop(0, blocks, advance, jnp.zeros(got.shape[1:], jnp.float32))
    incoming[me] = held[me]
    load.wait()
    rows_of = [pl.ds(k * half_f, half_f) for k in range(2)]

    def weight_copy(k, src, dst, by):
        return pltpu.make_async_remote_copy(
            src_ref=src,
            dst_ref=dst,
            send_sem=wsend.at[k],
            recv_sem=wrecv.at[k],
            device_id={"y": yy(by)},
            device_id_type=MESH,
        )

    sent = []
    for k, by in ((0, 1), (1, -1)):
        sent.append(weight_copy(k, weight, w.at[y], by))
        sent[-1].start()

    @pl.loop(1, blocks)
    def _(d):
        t = lax.rem(me + d, blocks)
        frm = lax.rem(me - d + blocks, blocks)
        state_copy(2, d, held.at[t], incoming.at[frm], t).wait()

    @pl.loop(0, seqs)
    def _(s):
        for h in range(heads):
            cols = pl.ds(h * head_dim, head_dim)
            pair = s * heads + h
            state = incoming[pair // per, lax.rem(pair, per)]
            carried = jnp.dot(q_ref[s, :, cols], state, preferred_element_type=jnp.float32)
            attended = inner[s, :, cols] + jnp.exp(cum_ref[:, h : h + 1]) * carried
            square = jnp.mean(attended * attended, axis=-1, keepdims=True)
            mixed = attended * lax.rsqrt(square + 1e-06) * scale[s, :, cols]
            parted = mixed.reshape(zs, cores, sub, head_dim)
            for k in range(cores):
                spread_tok[k, :, pl.ds(s, 1), :, cols] = parted[:, k : k + 1]

    own_tok[...] = spread_tok[...].reshape(own_tok.shape).astype(jnp.bfloat16)

    def copy(j, kind, src, dst, axis, to):
        return pltpu.make_async_remote_copy(
            src_ref=src,
            dst_ref=dst,
            send_sem=ssem.at[j, kind],
            recv_sem=rsem.at[j, kind],
            device_id={axis: to},
            device_id_type=MESH,
        )

    def send(*a):
        cp = copy(*a)
        cp.start()
        sent.append(cp)

    def arrived(j, kind, dst, axis):
        to = xs(1) if axis == "x" else zz(1) if axis == "z" else 1 - c
        copy(j, kind, dst, dst, axis, to).wait_recv()

    shift = (0, -1, 1, 2)
    send(0, 0, own_tok, tok.at[0], "x", xs(1))
    send(0, 1, own_tok, tok.at[1], "x", xs(-1))

    def dot_part(j, g):
        src = own_tok if j == 0 else tok.at[j - 1]
        cols = pl.ds(pl.multiple_of(g * block, 128), block)
        part = jnp.dot(src[...], w[g], preferred_element_type=jnp.float32)
        prod[j, :, :, :, cols] = part.reshape(cores, zs, count, block).astype(jnp.bfloat16)

    def near_groups(j):
        @pl.loop(0, n - 1)
        def _(i):
            dot_part(j, yy(i + i // 2))

    def exchange(j):
        send(j, 2, prod.at[j, 1 - c], other.at[j], "c", 1 - c)

    def core_add(j):
        arrived(j, 2, other.at[j], "c")
        mine = prod.at[j, c]

        @pl.loop(0, n)
        def _(b):
            cols = pl.ds(pl.multiple_of(b * block, 128), block)
            mine[:, :, cols] = (
                mine[:, :, cols].astype(jnp.float32) + other[j, :, :, cols].astype(jnp.float32)
            ).astype(jnp.bfloat16)

        for k in range(2):
            send(
                j,
                3 + k,
                mine.at[zz(2), :, pl.ds(k * half, half)],
                ring_opp.at[j, k],
                "z",
                zz(1 if k == 0 else -1),
            )

    def near(j):
        for k in range(2):
            arrived(j, 3 + k, ring_opp.at[j, k], "z")
            to = zz(1 if k == 0 else -1)
            mine = prod.at[j, c, to]
            cols = pl.ds(k * half, half)
            mine[:, cols] = (
                mine[:, cols].astype(jnp.float32) + ring_opp[j, k].astype(jnp.float32)
            ).astype(jnp.bfloat16)
            send(j, 5 + k, mine, ring_full.at[j, k], "z", to)

    def finish(j):
        for k in range(2):
            arrived(j, 5 + k, ring_full.at[j, k], "z")
        s = (
            prod[j, c, z].astype(jnp.float32)
            + ring_full[j, 0].astype(jnp.float32)
            + ring_full[j, 1].astype(jnp.float32)
        ).astype(jnp.bfloat16)
        if j == 0:
            out_ref[x] = s
        else:
            done[j] = s
            send(j, 7, done.at[j], out_ref.at[x], "x", xs(shift[j]))

    for k, by in ((0, 1), (1, -1)):
        weight_copy(k, weight, w.at[yy(-by)], by).wait_recv()
        part_w = w.at[yy(-by), rows_of[k]]
        sent.append(weight_copy(2 + k, part_w, part_w, by))
        sent[-1].start()
    near_groups(0)
    for k in range(2):
        arrived(0, k, tok.at[k], "x")
        cols = pl.ds(k * half_f, half_f)
        send(1, k, tok.at[k, :, cols], tok.at[2, :, cols], "x", xs(1 if k == 0 else -1))
    near_groups(1)
    for k, by in ((0, 1), (1, -1)):
        far_w = w.at[yy(2), rows_of[k]]
        weight_copy(2 + k, far_w, far_w, by).wait_recv()
    for j in range(2):
        dot_part(j, yy(2))
        exchange(j)
    near_groups(2)
    dot_part(2, yy(2))
    exchange(2)
    core_add(0)
    core_add(1)
    near(0)
    for k in range(2):
        arrived(1, k, tok.at[2, :, pl.ds(k * half_f, half_f)], "x")
    near_groups(3)
    dot_part(3, yy(2))
    exchange(3)
    core_add(2)
    near(1)
    core_add(3)
    finish(0)
    near(2)
    finish(1)
    near(3)
    finish(2)
    finish(3)
    for j in (1, 2, 3):
        arrived(j, 7, out_ref.at[xs(-shift[j])], "x")

    tokens, model = residual_ref.shape
    experts, main, _ = main_ref.shape
    total = jnp.zeros((tokens, 1), jnp.float32)
    for i in range(n):
        for k in range(n):
            cols = pl.ds((i * n + k) * block, block)
            r = stream_ref[:, :, cols].astype(jnp.float32).reshape(tokens, block)
            r = r + out_ref[k, :, pl.ds(i * block, block)].astype(jnp.float32)
            residual_ref[:, cols] = r
            total = total + jnp.sum(r * r, axis=-1, keepdims=True)
    inverse = lax.rsqrt(total / model + 1e-06)

    @pl.loop(0, n * n)
    def _(i):
        cols = pl.ds(pl.multiple_of(i * block, 128), block)
        normed = (residual_ref[:, cols] * inverse * norm_gain_ref[:, cols]).astype(jnp.bfloat16)
        placed = jnp.dot(slots_ref[...], normed, preferred_element_type=jnp.float32)
        main_ref[:, :, cols] = (
            placed[: experts * main].reshape(experts, main, block).astype(jnp.bfloat16)
        )
        last_ref[:, :, cols] = placed[experts * main :].reshape(experts, 1, block)

    for cp in sent:
        cp.wait_send()


def front(
    local_state,
    cumulative,
    queries,
    keys,
    values,
    out_gate,
    head_gain,
    out_weight,
    stream,
    norm_gain,
    slots,
    experts,
):
    n = 4
    seqs, heads, width, _ = local_state.shape
    blocks = n * n
    per = seqs * heads // blocks
    length, feats = queries.shape[1:]
    cores, zs = lax.axis_size("c"), lax.axis_size("z")
    count = seqs * length // (cores * zs)
    rows = seqs * length
    columns = out_weight.shape[1] * n
    model = stream.shape[2]
    bf16, f32 = jnp.bfloat16, jnp.float32
    chunks = local_state.reshape(blocks, per, width, width).astype(bf16)
    fades = jnp.broadcast_to(jnp.exp(cumulative[-1])[:, None, None], (heads, 8, width))
    vmem = pl.BlockSpec(memory_space=pltpu.VMEM)
    return pl.pallas_call(
        front_kernel,
        out_shape=[
            jax.ShapeDtypeStruct((count, model), f32),
            jax.ShapeDtypeStruct((experts, slots.shape[0] // experts - 1, model), bf16),
            jax.ShapeDtypeStruct((experts, 1, model), f32),
        ],
        in_specs=[vmem] * 12 + [pl.BlockSpec(memory_space=pl.ANY)],
        out_specs=[vmem] * 3,
        scratch_shapes=[
            pltpu.VMEM((n, count, columns), bf16),
            pltpu.VMEM(chunks.shape, bf16),
            pltpu.VMEM((blocks, per, 8, width), f32),
            pltpu.VMEM(chunks.shape, bf16),
            pltpu.VMEM(chunks.shape, bf16),
            pltpu.VMEM((heads, length, length), f32),
            pltpu.VMEM(queries.shape, f32),
            pltpu.VMEM(queries.shape, f32),
            pltpu.VMEM((cores, zs, seqs, length // (cores * zs), feats), f32),
            pltpu.VMEM((rows, feats), bf16),
            pltpu.VMEM((3, rows, feats), bf16),
            pltpu.VMEM((n, feats, columns // n), bf16),
            pltpu.VMEM((n, cores, zs, count, columns), bf16),
            pltpu.VMEM((n, zs, count, columns), bf16),
            pltpu.VMEM((n, 2, count, columns // 2), bf16),
            pltpu.VMEM((n, 2, count, columns), bf16),
            pltpu.VMEM((n, count, columns), bf16),
            pltpu.SemaphoreType.DMA((3, blocks)),
            pltpu.SemaphoreType.DMA((3, blocks)),
            pltpu.SemaphoreType.DMA((4,)),
            pltpu.SemaphoreType.DMA((4,)),
            pltpu.SemaphoreType.DMA((n, 8)),
            pltpu.SemaphoreType.DMA((n, 8)),
            pltpu.SemaphoreType.DMA((1,)),
        ],
        compiler_params=pltpu.CompilerParams(
            collective_id=3, has_side_effects=True, vmem_limit_bytes=56 << 20
        ),
        name="front",
    )(
        chunks,
        fades,
        queries,
        keys,
        values,
        out_gate,
        head_gain.reshape(1, feats),
        cumulative,
        cumulative.T,
        stream,
        norm_gain.reshape(1, model),
        slots,
        out_weight,
    )


def body(
    queries,
    keys,
    values,
    decay_log,
    out_gate,
    head_gain,
    out_weight,
    stream,
    norm_gain,
    expert_ids,
    expert_share,
    w_gate,
    w_up,
    w_down,
):
    seq_count, block_len, head_width = queries.shape
    head_count = decay_log.shape[1]
    head_dim = head_width // head_count
    split_shape = (seq_count, block_len, head_count, head_dim)
    key_heads = keys.reshape(split_shape)
    value_heads = values.reshape(split_shape)
    position = jnp.arange(block_len)
    causal = position[:, None] >= position[None, :]
    cumulative = jnp.sum(jnp.where(causal[:, :, None], decay_log[None], 0.0), axis=1)
    block_end = cumulative[-1]
    keys_faded = jnp.exp(block_end[None, :] - cumulative)[None, :, :, None] * key_heads.astype(
        jnp.float32
    )
    local_state = jnp.einsum(
        "sjhd,sjhe->shde",
        keys_faded.astype(jnp.bfloat16),
        value_heads,
        preferred_element_type=jnp.float32,
    )
    sub_len = stream.shape[1]
    model_width = stream.shape[2]
    exp_count = lax.axis_size(EXP)
    tok_count = seq_count * sub_len
    expert_count = exp_count
    capacity = max(2, (2 * tok_count + expert_count - 1) // expert_count + 1)
    slot_total = expert_count * capacity
    picks = expert_ids.reshape(2 * tok_count)
    copy_no = jnp.arange(2 * tok_count)
    earlier = (copy_no[None, :] < copy_no[:, None]) & (picks[None, :] == picks[:, None])
    ranking = jnp.sum(earlier.astype(jnp.int32), axis=1)
    main = capacity - 1
    slot_of = jnp.where(ranking < main, picks * main + ranking, expert_count * main + picks)
    placing = slot_of[:, None] == jnp.arange(slot_total, dtype=jnp.int32)[None, :]
    token_placing = jnp.any(placing.reshape(tok_count, 2, slot_total), axis=1)
    main_total = expert_count * main
    residual_sum, main_rows, last_rows = front(
        local_state,
        cumulative,
        queries,
        keys,
        values,
        out_gate,
        head_gain,
        out_weight,
        stream,
        norm_gain,
        token_placing.T.astype(jnp.bfloat16),
        expert_count,
    )
    hid = expert_terms(main_rows, last_rows, w_gate[0].T, w_up[0].T)
    back_main, back_last = expert_sum(hid, w_down[0], expert_count)
    returned = jnp.concatenate(
        [
            back_main.reshape(main_total, model_width).astype(jnp.float32),
            back_last.reshape(expert_count, model_width),
        ],
        axis=0,
    )
    weighting = jnp.where(placing, expert_share.reshape(2 * tok_count, 1), 0.0)
    weighting = jnp.sum(weighting.reshape(tok_count, 2, slot_total), axis=1)
    expert_mix = jnp.dot(weighting, returned, precision=lax.Precision.HIGHEST)
    result = (residual_sum + expert_mix).astype(jnp.bfloat16)
    return result.reshape(seq_count, sub_len, model_width)


def solution(mesh):
    n_exp = mesh.shape["exp"]
    side = round(mesh.shape["ctx"] ** 0.5)
    fine = Mesh(mesh.devices.reshape(side, side, n_exp // 2, 2), ("y", "x", "z", "c"))
    return jax.shard_map(
        body,
        mesh=fine,
        in_specs=(
            P(None, CTX, EXP),
            P(None, CTX, EXP),
            P(None, CTX, EXP),
            P(CTX, EXP),
            P(None, CTX, EXP),
            P(EXP),
            P(EXP, CTX),
            P(None, CTX + EXP, None),
            P(),
            P(CTX + EXP, None, None),
            P(CTX + EXP, None, None),
            P(EXP, None, CTX),
            P(EXP, None, CTX),
            P(EXP, CTX, None),
        ),
        out_specs=P(None, CTX + EXP, None),
        check_vma=False,
    )
```

profile of v0, /device:TPU:1, one launch (start us, length us, event | category | flops | bytes accessed | tf_op | source)
XLA Modules:
  0.0 311.4 jit_solution(1318935541996826328)
XLA Ops:
  0.0 0.0 copy-start.4
  0.0 0.8 select_reduce_fusion.cum_ref
  0.9 0.0 copy-start.1
  0.9 0.1 copy.40
  0.9 0.0 copy-start.3
  0.9 0.1 subtract_exponential_fusion
  1.0 2.8 convolution_convert_fusion
  3.8 0.0 copy-done.4
  3.8 0.1 copy.45
  3.9 0.1 copy.46
  4.0 0.1 copy.44
  4.1 0.1 eq.30
  4.2 0.2 convert_reduce_fusion
  4.4 0.1 reduce_sum.31
  4.5 0.1 copy.47
  4.6 0.1 fusion.10
  4.7 0.7 copy.48
  5.4 0.7 broadcast_in_dim.52.fades
  6.1 0.0 copy-done.1
  6.1 0.0 copy-done.3
  6.1 94.3 %front.1 = (f32[32,6144]{1,0:T(8,128)}, bf16[8,8,6144]{2,1,0:T(8,128)(2,1)}, f32[8,1,6144]{2,1,0:T(1,128)}) custom-call(bf16[16,2,128,128]{3,2,1,0:T(8,128)(2,1)} %bitcast.49, f32[8,8,128]{2,1,0:T(8,128)} %broadcast_in_dim.52.fades, bf16[4,64,1024]{2,1,0:T(8,128)(2,1)} %q_ref.1, bf16[4,64,1024]{2,1,0:T(8,128)(2,1)} %k_ref.1, bf16[4,64,1024]{2,1,0:T(8,128)(2,1)} %v_ref.1, ...), custom_call_target="tpu_custom_call" | custom-call | tf_op jit(solution)/shard_map/front/pallas_call | solution.py:930
  100.4 109.7 %gather_experts.1 = (f32[4,4,72,576]{3,2,1,0:T(8,128)}, bf16[4,288,3072]{2,1,0:T(8,128)(2,1)}, bf16[4,288,3072]{2,1,0:T(8,128)(2,1)}, bf16[72,6144]{1,0:T(8,128)(2,1)}) custom-call(bf16[8,8,6144]{2,1,0:T(8,128)(2,1)} %get-tuple-element.12.main_ref, f32[8,1,6144]{2,1,0:T(1,128)} %get-tuple-element.13.last_ref, bf16[576,6144]{1,0:T(8,128)(2,1)} %bitcast.47, ...), custom_call_target="tpu_custom_call" | custom-call | tf_op jit(solution)/shard_map/gather_experts/pallas_call | solution.py:493
  210.1 97.9 %sum_experts.1 = (bf16[8,8,6144]{2,1,0:T(8,128)(2,1)}, f32[8,1,6144]{2,1,0:T(1,128)}) custom-call(f32[4,4,72,576]{3,2,1,0:T(8,128)} %get-tuple-element.14.hid_ref, bf16[576,6144]{1,0:T(8,128)(2,1)} %bitcast.46), custom_call_target="tpu_custom_call" | custom-call | tf_op jit(solution)/shard_map/sum_experts/pallas_call | solution.py:533
  308.1 0.0 copy-start.2
  308.1 0.0 copy-start.5
  308.1 0.0 copy-start
  308.1 1.3 bitcast_convert_fusion
  309.4 0.0 copy-done.2
  309.4 0.1 copy.59
  309.5 0.0 copy-done.5
  309.5 0.1 select_reduce_fusion.1
  309.6 0.0 copy-done
  309.6 1.7 fusion.1
  (6 shorter events, 0.0 us)
Async XLA Ops:
  0.0 3.8 %copy-start.4 = (s32[1,32,2]{1,2,0:T(2,128)S(1)}, s32[1,32,2]{1,2,0:T(2,128)}, u32[]{:S(2)}) copy-start(s32[1,32,2]{1,2,0:T(2,128)} %param.23) | copy-start | bytes 772
  0.9 5.3 %copy-start.1 = (f32[64,8]{1,0:T(8,128)}, f32[64,8]{1,0:T(8,128)S(1)}, u32[]{:S(2)}) copy-start(f32[64,8]{1,0:T(8,128)S(1)} %select_reduce_fusion.cum_ref) | copy-start | bytes 6148
  0.9 5.2 %copy-start.3 = (f32[64,8]{0,1:T(8,128)}, f32[64,8]{0,1:T(8,128)S(1)}, u32[]{:S(2)}) copy-start(f32[64,8]{0,1:T(8,128)S(1)} %copy.40) | copy-start | bytes 6148
  308.1 1.4 copy-start.2
  308.1 1.4 copy-start.5
  308.1 1.5 copy-start
where the time goes:
time: 312 us; the launch traced here: 311 us
  Pallas kernels  302 us (97%)
  matrix products  4.58 us (1%)
    pallas_call x1, Pallas kernels, expert_terms(): pl.pallas_call(gather_kernel, out_shape=[jax.ShapeDtypeStruct((n, n, coun...  110 us
    pallas_call x1, Pallas kernels, expert_sum(): pl.pallas_call(reduce_kernel, out_shape=[jax.ShapeDtypeStruct((experts, m...  97.9 us
    pallas_call x1, Pallas kernels, front(): pl.pallas_call(front_kernel, out_shape=[jax.ShapeDtypeStruct((count, mode...  94.3 us

commit v1 on v0

--- a/solution.py
+++ b/solution.py
@@ -89,14 +89,19 @@
                 device_id_type=MESH,
             )
             for k, (src, dst) in enumerate(
-                ((main_ref.at[to], main_rows(frm)), (last_ref.at[to], last_in.at[frm]))
+                (
+                    (main_ref.at[to, :, pl.ds(0, half)], main_rows(frm).at[:, pl.ds(0, half)]),
+                    (last_ref.at[to], last_in.at[frm]),
+                    (main_ref.at[to, :, pl.ds(half, half)], main_rows(frm).at[:, pl.ds(half, half)]),
+                )
             )
         ]
 
-    @pl.loop(1, experts)
-    def _(d):
-        for c in deal(d, lax.rem(mine_e + d, experts), mine_e):
-            c.start()
+    for k in (1, 0, 2):
+
+        @pl.loop(1, experts)
+        def _(d):
+            deal(d, lax.rem(mine_e + d, experts), mine_e)[k].start()
 
     own_main = pltpu.make_async_copy(main_ref.at[mine_e], main_rows(mine_e), lsem.at[6])
     own_last = pltpu.make_async_copy(last_ref.at[mine_e], last_in.at[mine_e], lsem.at[7])
@@ -107,17 +112,20 @@
     own_main.wait()
     own_last.wait()
 
-    @pl.loop(1, experts)
-    def _(d):
-        for c in deal(d, lax.rem(mine_e + d, experts), lax.rem(mine_e - d + experts, experts)):
-            c.wait()
-
+    def dealt(k):
+        @pl.loop(1, experts)
+        def _(d):
+            to, frm = lax.rem(mine_e + d, experts), lax.rem(mine_e - d + experts, experts)
+            deal(d, to, frm)[k].wait()
+
+    dealt(1)
     last_out[...] = last_in[...].reshape(last_out.shape).astype(jnp.bfloat16)
     put_last = pltpu.make_async_copy(
         last_out, rows_ref.at[pl.ds(experts * main, experts)], lsem.at[6]
     )
     put_last.start()
     put_last.wait()
+    dealt(0)
 
     def row(h, fi, si):
         return buf[h].at[fi, pl.ds(pl.multiple_of(si * count, 8), count)]
@@ -155,11 +163,10 @@
     for h in range(2):
         first, second = AXES[h]
         mine = row(h, place[first], place[second])
+        if h == 1:
+            dealt(2)
         for kind in range(2):
             send(h, n, kind, first, own[h], mine)
-    for h in range(2):
-        first, second = AXES[h]
-        mine = row(h, place[first], place[second])
         for kind in range(2):
             send(h, 0, kind, second, own[h], mine)
         keep.append(pltpu.make_async_copy(own[h], mine, lsem.at[2 + h]))
@@ -239,8 +246,11 @@
                 keep[h].wait()
             far(h, j)
             load(h, j).start()
-        for h in range(2):
-            multiply(h, j)
+            if j == n - 1:
+                multiply(h, j)
+        if j < n - 1:
+            for h in range(2):
+                multiply(h, j)
         if j == 2:
 
             @pl.loop(0, 9)
@@ -511,8 +521,8 @@
             pltpu.SemaphoreType.DMA((2, n + 1, 4)),
             pltpu.SemaphoreType.DMA((2, n + 1, 4)),
             pltpu.SemaphoreType.DMA((8,)),
-            pltpu.SemaphoreType.DMA((2, experts)),
-            pltpu.SemaphoreType.DMA((2, experts)),
+            pltpu.SemaphoreType.DMA((3, experts)),
+            pltpu.SemaphoreType.DMA((3, experts)),
         ],
         compiler_params=pltpu.CompilerParams(
             collective_id=1, has_side_effects=True, vmem_limit_bytes=60 << 20

time: 312 us -> 312 us (level)
  no operation moved by 1% of the time
where the time goes in v1:
time: 312 us
  Pallas kernels  302 us (97%)
  matrix products  4.58 us (1%)
    pallas_call x1, Pallas kernels, expert_terms(): pl.pallas_call(gather_kernel, out_shape=[jax.ShapeDtypeStruct((n, n, coun...  110 us
    pallas_call x1, Pallas kernels, expert_sum(): pl.pallas_call(reduce_kernel, out_shape=[jax.ShapeDtypeStruct((experts, m...  98.1 us
    pallas_call x1, Pallas kernels, front(): pl.pallas_call(front_kernel, out_shape=[jax.ShapeDtypeStruct((count, mode...  94.3 us

profile of v1, /device:TPU:1, one launch (start us, length us, event | category | flops | bytes accessed | tf_op | source)
XLA Modules:
  0.0 311.8 jit_solution(4646873356715361980)
XLA Ops:
  0.0 0.0 copy-start.4
  0.0 0.8 select_reduce_fusion.cum_ref
  0.9 0.0 copy-start.1
  0.9 0.1 copy.40
  0.9 0.0 copy-start.3
  0.9 0.1 subtract_exponential_fusion
  1.0 2.8 convolution_convert_fusion
  3.8 0.0 copy-done.4
  3.8 0.1 copy.45
  3.9 0.1 copy.46
  4.0 0.1 copy.44
  4.1 0.1 eq.30
  4.2 0.2 convert_reduce_fusion
  4.4 0.1 reduce_sum.31
  4.5 0.1 copy.47
  4.6 0.1 fusion.10
  4.7 0.7 copy.48
  5.4 0.7 broadcast_in_dim.52.fades
  6.1 0.0 copy-done.1
  6.1 0.0 copy-done.3
  6.1 94.3 %front.1 = (f32[32,6144]{1,0:T(8,128)}, bf16[8,8,6144]{2,1,0:T(8,128)(2,1)}, f32[8,1,6144]{2,1,0:T(1,128)}) custom-call(bf16[16,2,128,128]{3,2,1,0:T(8,128)(2,1)} %bitcast.49, f32[8,8,128]{2,1,0:T(8,128)} %broadcast_in_dim.52.fades, bf16[4,64,1024]{2,1,0:T(8,128)(2,1)} %q_ref.1, bf16[4,64,1024]{2,1,0:T(8,128)(2,1)} %k_ref.1, bf16[4,64,1024]{2,1,0:T(8,128)(2,1)} %v_ref.1, ...), custom_call_target="tpu_custom_call" | custom-call | tf_op jit(solution)/shard_map/front/pallas_call | solution.py:940
  100.4 109.9 %gather_experts.1 = (f32[4,4,72,576]{3,2,1,0:T(8,128)}, bf16[4,288,3072]{2,1,0:T(8,128)(2,1)}, bf16[4,288,3072]{2,1,0:T(8,128)(2,1)}, bf16[72,6144]{1,0:T(8,128)(2,1)}) custom-call(bf16[8,8,6144]{2,1,0:T(8,128)(2,1)} %get-tuple-element.12.main_ref, f32[8,1,6144]{2,1,0:T(1,128)} %get-tuple-element.13.last_ref, bf16[576,6144]{1,0:T(8,128)(2,1)} %bitcast.47, ...), custom_call_target="tpu_custom_call" | custom-call | tf_op jit(solution)/shard_map/gather_experts/pallas_call | solution.py:503
  210.4 98.1 %sum_experts.1 = (bf16[8,8,6144]{2,1,0:T(8,128)(2,1)}, f32[8,1,6144]{2,1,0:T(1,128)}) custom-call(f32[4,4,72,576]{3,2,1,0:T(8,128)} %get-tuple-element.14.hid_ref, bf16[576,6144]{1,0:T(8,128)(2,1)} %bitcast.46), custom_call_target="tpu_custom_call" | custom-call | tf_op jit(solution)/shard_map/sum_experts/pallas_call | solution.py:543
  308.5 0.0 copy-start.2
  308.5 0.0 copy-start.5
  308.5 0.0 copy-start
  308.5 1.3 bitcast_convert_fusion
  309.8 0.0 copy-done.2
  309.9 0.1 copy.59
  309.9 0.0 copy-done.5
  309.9 0.1 select_reduce_fusion.1
  310.0 0.0 copy-done
  310.0 1.7 fusion.1
  (6 shorter events, 0.0 us)
Async XLA Ops:
  0.0 3.8 %copy-start.4 = (s32[1,32,2]{1,2,0:T(2,128)S(1)}, s32[1,32,2]{1,2,0:T(2,128)}, u32[]{:S(2)}) copy-start(s32[1,32,2]{1,2,0:T(2,128)} %param.23) | copy-start | bytes 772
  0.9 5.3 %copy-start.1 = (f32[64,8]{1,0:T(8,128)}, f32[64,8]{1,0:T(8,128)S(1)}, u32[]{:S(2)}) copy-start(f32[64,8]{1,0:T(8,128)S(1)} %select_reduce_fusion.cum_ref) | copy-start | bytes 6148
  0.9 5.2 %copy-start.3 = (f32[64,8]{0,1:T(8,128)}, f32[64,8]{0,1:T(8,128)S(1)}, u32[]{:S(2)}) copy-start(f32[64,8]{0,1:T(8,128)S(1)} %copy.40) | copy-start | bytes 6148
  308.5 1.4 copy-start.2
  308.5 1.4 copy-start.5
  308.5 1.5 copy-start

commit v2 on v1

--- a/solution.py
+++ b/solution.py
@@ -332,14 +332,14 @@
     def arrived(h, stage, kind, axis, dst):
         copy(h, stage, kind, axis, dst, dst).wait_recv()
 
-    def multiply(h, j):
+    def multiply(h, j, k):
         lead = step(AXES[h][0], shift[j])
         taken = hid_ref[lead] if h == 0 else hid_ref[:, pl.ds(lead, 1)]
         rows[...] = taken.reshape(rows.shape).astype(jnp.bfloat16)
 
-        @pl.loop(0, half // block)
+        @pl.loop(0, quarter // block)
         def _(b):
-            at = pl.multiple_of(b * block, 128)
+            at = pl.multiple_of(k * quarter + b * block, 128)
             got = jnp.dot(
                 rows[...],
                 wd[:, pl.ds(pl.multiple_of(h * half + at, 128), block)],
@@ -347,17 +347,10 @@
             )
             t[h][j, :, :, pl.ds(at, block)] = got.reshape(n, count, block).astype(jnp.bfloat16)
 
-    def far_out(h, j):
+    def far_out(h, j, k):
         ring = AXES[h][1]
-        for k in range(2):
-            send(
-                h,
-                j,
-                k,
-                ring,
-                t[h].at[j, step(ring, 2), :, pl.ds(k * quarter, quarter)],
-                r_opp.at[h, j, k],
-            )
+        src = t[h].at[j, step(ring, 2), :, pl.ds(k * quarter, quarter)]
+        send(h, j, k, ring, src, r_opp.at[h, j, k])
 
     def add_to(ref, k, other):
         @pl.loop(0, quarter // block)
@@ -426,18 +419,20 @@
         )
 
     for j in range(2):
-        for h in range(2):
-            multiply(h, j)
-            if j == 0 and h == 0:
-                pl.semaphore_wait(barrier, len(others))
-            far_out(h, j)
+        for k in range(2):
+            for h in range(2):
+                multiply(h, j, k)
+                if j == 0 and h == 0 and k == 0:
+                    pl.semaphore_wait(barrier, len(others))
+                far_out(h, j, k)
     for j in range(n):
         for h in range(2):
             near(h, j)
         if j + 2 < n:
-            for h in range(2):
-                multiply(h, j + 2)
-                far_out(h, j + 2)
+            for k in range(2):
+                for h in range(2):
+                    multiply(h, j + 2, k)
+                    far_out(h, j + 2, k)
         if j == 1:
             for h in range(2):
                 finish(h, 0)

time: 312 us -> 316 us (1.013); the launches traced: 312 us -> 311 us
  no operation moved by 1% of the time
where the time goes in v2:
time: 316 us; the launch traced here: 311 us
  Pallas kernels  301 us (95%)
  matrix products  4.58 us (1%)
    pallas_call x1, Pallas kernels, expert_terms(): pl.pallas_call(gather_kernel, out_shape=[jax.ShapeDtypeStruct((n, n, coun...  110 us
    pallas_call x1, Pallas kernels, expert_sum(): pl.pallas_call(reduce_kernel, out_shape=[jax.ShapeDtypeStruct((experts, m...  96.8 us
    pallas_call x1, Pallas kernels, front(): pl.pallas_call(front_kernel, out_shape=[jax.ShapeDtypeStruct((count, mode...  94.4 us

profile of v2, /device:TPU:1, one launch (start us, length us, event | category | flops | bytes accessed | tf_op | source)
XLA Modules:
  0.0 310.9 jit_solution(4929781255703192247)
XLA Ops:
  0.0 0.0 copy-start.4
  0.0 0.8 select_reduce_fusion.cum_ref
  0.9 0.0 copy-start.1
  0.9 0.1 copy.40
  0.9 0.0 copy-start.3
  0.9 0.1 subtract_exponential_fusion
  1.0 2.8 convolution_convert_fusion
  3.8 0.0 copy-done.4
  3.8 0.1 copy.45
  3.9 0.1 copy.46
  4.0 0.1 copy.44
  4.1 0.1 eq.30
  4.2 0.2 convert_reduce_fusion
  4.4 0.1 reduce_sum.31
  4.5 0.1 copy.47
  4.6 0.1 fusion.10
  4.7 0.7 copy.48
  5.4 0.7 broadcast_in_dim.52.fades
  6.1 0.0 copy-done.1
  6.1 0.0 copy-done.3
  6.1 94.4 %front.1 = (f32[32,6144]{1,0:T(8,128)}, bf16[8,8,6144]{2,1,0:T(8,128)(2,1)}, f32[8,1,6144]{2,1,0:T(1,128)}) custom-call(bf16[16,2,128,128]{3,2,1,0:T(8,128)(2,1)} %bitcast.49, f32[8,8,128]{2,1,0:T(8,128)} %broadcast_in_dim.52.fades, bf16[4,64,1024]{2,1,0:T(8,128)(2,1)} %q_ref.1, bf16[4,64,1024]{2,1,0:T(8,128)(2,1)} %k_ref.1, bf16[4,64,1024]{2,1,0:T(8,128)(2,1)} %v_ref.1, ...), custom_call_target="tpu_custom_call" | custom-call | tf_op jit(solution)/shard_map/front/pallas_call | solution.py:935
  100.5 109.9 %gather_experts.1 = (f32[4,4,72,576]{3,2,1,0:T(8,128)}, bf16[4,288,3072]{2,1,0:T(8,128)(2,1)}, bf16[4,288,3072]{2,1,0:T(8,128)(2,1)}, bf16[72,6144]{1,0:T(8,128)(2,1)}) custom-call(bf16[8,8,6144]{2,1,0:T(8,128)(2,1)} %get-tuple-element.12.main_ref, f32[8,1,6144]{2,1,0:T(1,128)} %get-tuple-element.13.last_ref, bf16[576,6144]{1,0:T(8,128)(2,1)} %bitcast.47, ...), custom_call_target="tpu_custom_call" | custom-call | tf_op jit(solution)/shard_map/gather_experts/pallas_call | solution.py:498
  210.4 96.8 %sum_experts.1 = (bf16[8,8,6144]{2,1,0:T(8,128)(2,1)}, f32[8,1,6144]{2,1,0:T(1,128)}) custom-call(f32[4,4,72,576]{3,2,1,0:T(8,128)} %get-tuple-element.14.hid_ref, bf16[576,6144]{1,0:T(8,128)(2,1)} %bitcast.46), custom_call_target="tpu_custom_call" | custom-call | tf_op jit(solution)/shard_map/sum_experts/pallas_call | solution.py:538
  307.1 0.0 copy-start.2
  307.1 0.0 copy-start.5
  307.2 0.0 copy-start
  307.2 1.3 bitcast_convert_fusion
  308.5 0.0 copy-done.2
  308.5 0.1 copy.59
  308.6 0.0 copy-done.5
  308.6 0.1 select_reduce_fusion.1
  308.7 0.0 copy-done
  308.7 1.7 fusion.1
  (6 shorter events, 0.0 us)
Async XLA Ops:
  0.0 3.8 %copy-start.4 = (s32[1,32,2]{1,2,0:T(2,128)S(1)}, s32[1,32,2]{1,2,0:T(2,128)}, u32[]{:S(2)}) copy-start(s32[1,32,2]{1,2,0:T(2,128)} %param.23) | copy-start | bytes 772
  0.9 5.3 %copy-start.1 = (f32[64,8]{1,0:T(8,128)}, f32[64,8]{1,0:T(8,128)S(1)}, u32[]{:S(2)}) copy-start(f32[64,8]{1,0:T(8,128)S(1)} %select_reduce_fusion.cum_ref) | copy-start | bytes 6148
  0.9 5.2 %copy-start.3 = (f32[64,8]{0,1:T(8,128)}, f32[64,8]{0,1:T(8,128)S(1)}, u32[]{:S(2)}) copy-start(f32[64,8]{0,1:T(8,128)S(1)} %copy.40) | copy-start | bytes 6148
  307.1 1.4 copy-start.2
  307.1 1.4 copy-start.5
  307.2 1.5 copy-start
